TPU v7x, 32 devices: a whole 2x2x4 slice. The times are simulated.
32 devices in a mesh: tm: 2 (over x), vox: 8 (over z, y), feat: 2 (over core).
Axes of the slice: x: 2, y: 2, z: 4, core: 2. Of those that a mesh axis runs over, the one named last changes fastest.
Arguments:
- design_matrix: bfloat16 [256, 4096], P(None, ('tm', 'feat')), may hold values from -6 to 6
- measured_signals: bfloat16 [256, 16384], P('tm', 'vox'), may hold values from -6 to 6
- predictor_group_label: int32 [4096], P('vox'), may hold values from 0 to 3
- shrinkage_weights: float32 [2, 4], replicated, may hold values from 0.1 to 10
- target_shrink_choice: int32 [256], P('vox'), may hold values from 0 to 1
Outputs:
- trailing: float32 [2, 4096, 4096], P(None, ('tm', 'feat'), 'vox')
- right_sides: float32 [4096, 16384], P(('tm', 'feat'), 'vox')
All inputs are finite; a program needn't handle non-finite values.
Results may differ from a plain program's by a relative error of at most 0.0003.
Values may be sent and summed in bfloat16 or wider, within the bound.
No kernel may reach another device: no remote copies, remote signals or barrier semaphores. Data moves between devices by JAX's collectives and lax.ppermute only.
A program may use at most 128 MiB of HBM per device.

v0:
```python
import math

import jax
import jax.numpy as jnp
from jax import lax
from jax.sharding import PartitionSpec as P

P_SIZE = 4096
PREDICTOR_GROUPS = 4
SHRINK_OPTIONS = 2
GROUP = 64


def spread(block, axis, owner):
    block = jnp.where(lax.axis_index(axis) == owner, block, jnp.zeros_like(block))
    return lax.psum(block, axis)


def local(
    design_matrix, measured_signals, predictor_group_label, shrinkage_weights, target_shrink_choice
):
    row_index = lax.axis_index(("tm", "feat"))
    column_index = lax.axis_index("vox")
    total_time, row_block = design_matrix.shape
    column_width = P_SIZE // lax.axis_size("vox")
    voxel_count = measured_signals.shape[1]
    source_row = column_index * column_width // row_block
    own_columns = lax.dynamic_slice_in_dim(
        design_matrix, column_index * column_width - source_row * row_block, column_width, 1
    )
    shared_columns = spread(own_columns, ("tm", "feat"), source_row)
    gram_tile = (
        jnp.einsum("tr,tc->rc", design_matrix, shared_columns, preferred_element_type=jnp.float32)
        / total_time
    )
    global_rows = row_index * row_block + jnp.arange(row_block)
    global_columns = column_index * column_width + jnp.arange(column_width)
    group_membership_mask = (
        predictor_group_label[:, None] == jnp.arange(PREDICTOR_GROUPS)[None, :]
    ).astype(jnp.float32)
    predictor_shrinkage = jnp.dot(
        shrinkage_weights, group_membership_mask.T, precision=lax.Precision.HIGHEST
    )
    on_diagonal = (global_rows[:, None] == global_columns[None, :])[None, :, :]
    system_tiles = gram_tile[None, :, :] + jnp.where(
        on_diagonal, predictor_shrinkage[:, None, :], 0.0
    )
    right_sides = jnp.einsum(
        "tr,tv->rv",
        design_matrix,
        lax.all_gather(measured_signals, "tm", axis=0, tiled=True),
        preferred_element_type=jnp.float32,
    )
    right_sides = right_sides / math.sqrt(total_time)
    first_ridge = jnp.repeat(target_shrink_choice, GROUP) == 0
    identity_block = jnp.broadcast_to(
        jnp.eye(column_width, dtype=jnp.float32), (SHRINK_OPTIONS, column_width, column_width)
    )
    diagonal_owner = 0 // row_block
    local_offset = 0 - diagonal_owner * row_block
    diagonal = system_tiles[:, local_offset : local_offset + column_width, :]
    diagonal = spread(diagonal, ("tm", "feat"), diagonal_owner)
    diagonal = jnp.where(column_index == 0, diagonal, identity_block)
    factor = jnp.linalg.cholesky(diagonal)
    solved = lax.linalg.triangular_solve(
        factor, system_tiles, left_side=False, lower=True, transpose_a=True
    )
    solved = jnp.where((global_rows >= 0)[None, :, None], solved, 0.0)
    panel, factor = (spread(solved, "vox", 0), spread(factor, "vox", 0))
    panel_slice = lax.dynamic_slice_in_dim(
        panel, column_index * column_width - source_row * row_block, column_width, 1
    )
    partner_rows = spread(panel_slice, ("tm", "feat"), source_row)
    block_sides = jnp.broadcast_to(
        right_sides[local_offset : local_offset + column_width],
        (SHRINK_OPTIONS, column_width, voxel_count),
    )
    solutions = lax.linalg.triangular_solve(factor, block_sides, left_side=True, lower=True)
    solved_sides = jnp.where(first_ridge[None, :], solutions[0], solutions[1])
    solved_sides = spread(solved_sides, ("tm", "feat"), diagonal_owner)
    system_tiles = system_tiles - jnp.einsum(
        "brk,bck->brc", panel, partner_rows, precision=lax.Precision.HIGHEST
    )
    update_first = jnp.dot(panel[0], solved_sides, precision=lax.Precision.HIGHEST)
    update_second = jnp.dot(panel[1], solved_sides, precision=lax.Precision.HIGHEST)
    right_sides = right_sides - jnp.where(first_ridge[None, :], update_first, update_second)
    inside_block = (global_rows >= 0) & (global_rows < column_width)
    placed = (
        jnp.zeros((row_block, voxel_count), jnp.float32)
        .at[local_offset : local_offset + column_width]
        .set(solved_sides)
    )
    right_sides = jnp.where(inside_block[:, None], placed, right_sides)
    return (system_tiles, right_sides)


def solution(mesh):
    return jax.shard_map(
        local,
        mesh=mesh,
        in_specs=(P(None, ("tm", "feat")), P("tm", "vox"), P("vox"), P(), P("vox")),
        out_specs=(P(None, ("tm", "feat"), "vox"), P(("tm", "feat"), "vox")),
        check_vma=False,
    )
```

profile of v0, /device:TPU:0, one launch (start us, length us, event | category | flops | bytes accessed | tf_op | source)
XLA Modules:
  0.0 928.3 jit_solution(13369854478591453120)
XLA Ops:
  11.3 35.5 %all-reduce.9.cloned.1.call-done = bf16[256,512]{1,0:T(8,128)(2,1)} async-done(((bf16[256,512]{1,0:T(8,128)(2,1)}), bf16[256,512]{1,0:T(8,128)(2,1)}) %all-reduce.9.cloned.1.call-update) | async-done | bytes 262160 | tf_op jit(solution)/shard_map/psum | solution.py:16
  48.8 2.0 copy-done.5
  54.0 61.2 %all-reduce.11.cloned.1.call-done = f32[2,512,512]{1,2,0:T(8,128)} async-done(((f32[2,512,512]{1,2,0:T(8,128)}), f32[2,512,512]{1,2,0:T(8,128)}) %all-reduce.11.cloned.1.call-update) | async-done | bytes 2097168 | tf_op jit(solution)/shard_map/psum | solution.py:16
  115.3 3.3 broadcast_select_fusion
  118.6 3.1 copy.45
  121.7 2.9 fusion.30
  125.9 23.5 %custom-call.37 = f32[2,128,128]{2,1,0:T(8,128)S(1)} custom-call(f32[2,128,128]{2,1,0:T(8,128)S(1)} %cholesky.271), custom_call_target="Cholesky" | custom-call | tf_op jit(solution)/shard_map/jit(cholesky)/cholesky | solution.py:64
  149.4 19.7 %custom-call.38 = f32[2,1,128,128]{2,3,1,0:T(8,128)S(1)} custom-call(f32[2,1,128,128]{3,2,1,0:T(8,128)S(1)} %select_bitcast_fusion.2), custom_call_target="InvertDiagBlocksLowerTriangular" | custom-call | tf_op jit(solution)/shard_map/jit(cholesky)/cholesky | solution.py:64
  170.6 2.3 convolution_subtract_fusion.3
  174.7 24.3 %custom-call.39 = f32[2,128,128]{2,1,0:T(8,128)S(1)} custom-call(f32[2,128,128]{2,1,0:T(8,128)} %cholesky.275), custom_call_target="Cholesky" | custom-call | tf_op jit(solution)/shard_map/jit(cholesky)/cholesky | solution.py:64
  201.2 21.5 %custom-call.40 = f32[2,1,128,128]{2,3,1,0:T(8,128)} custom-call(f32[2,1,128,128]{3,2,1,0:T(8,128)} %select_bitcast_fusion.1), custom_call_target="InvertDiagBlocksLowerTriangular" | custom-call | tf_op jit(solution)/shard_map/jit(cholesky)/cholesky | solution.py:64
  225.4 2.0 convolution_subtract_fusion.4
  227.4 23.5 %custom-call.41 = f32[2,128,128]{2,1,0:T(8,128)S(1)} custom-call(f32[2,128,128]{2,1,0:T(8,128)S(1)} %cholesky.280), custom_call_target="Cholesky" | custom-call | tf_op jit(solution)/shard_map/jit(cholesky)/cholesky | solution.py:64
  251.7 19.7 %custom-call.42 = f32[2,1,128,128]{2,3,1,0:T(8,128)S(1)} custom-call(f32[2,1,128,128]{3,2,1,0:T(8,128)S(1)} %select_bitcast_fusion), custom_call_target="InvertDiagBlocksLowerTriangular" | custom-call | tf_op jit(solution)/shard_map/jit(cholesky)/cholesky | solution.py:64
  272.4 2.0 convolution_subtract_fusion.5
  274.4 23.5 %custom-call.43 = f32[2,128,128]{2,1,0:T(8,128)S(1)} custom-call(f32[2,128,128]{2,1,0:T(8,128)S(1)} %convolution_subtract_fusion.5), custom_call_target="Cholesky" | custom-call | tf_op jit(solution)/shard_map/jit(cholesky)/cholesky | solution.py:64
  299.0 4.3 fusion.31
  303.4 13.0 %while.3 = (s32[]{:T(128)}, f32[2,512,512]{1,2,0:T(8,128)}, s32[4,2]{0,1:T(2,128)S(1)}, f32[4,2,128,128]{3,2,0,1:T(8,128)S(1)}, s32[]{:T(128)}) while((s32[]{:T(128)}, f32[2,512,512]{1,2,0:T(8,128)}, s32[4,2]{0,1:T(2,128)S(1)}, f32[4,2,128,128]{3,2,0,1:T(8,128)S(1)}, s32[]{:T(128)}) %tuple.56), condition=%wide.while_cond.1, body=%wide.while_body.1.sunk | while | flops 2 | bytes 786541 | solution.py:65
  304.1 2.4 constant_dynamic-slice_fusion.9
  307.3 2.4 constant_dynamic-slice_fusion.9
  310.6 2.4 constant_dynamic-slice_fusion.9
  313.9 2.4 constant_dynamic-slice_fusion.9
  316.4 78.8 %custom-call.44 = f32[2,4,128,128]{2,3,1,0:T(8,128)S(1)} custom-call(f32[2,4,128,128]{3,2,1,0:T(8,128)S(1)} %bitcast.114), custom_call_target="InvertDiagBlocksLowerTriangular" | custom-call | tf_op jit(solution)/shard_map/triangular_solve | solution.py:65
  395.2 2.3 fusion.39
  397.5 2.5 convolution_subtract_fusion.2
  401.1 2.3 fusion.33
  404.6 3.2 fusion.36
  408.9 3.0 fusion.8
  412.9 2.5 convolution_multiply_fusion
  415.5 3.4 copy-done.2
  420.6 199.6 %all-reduce.13.cloned.1.call-done = (f32[2,1024,512]{1,2,0:T(8,128)}, f32[2,512,512]{1,2,0:T(8,128)}) async-done(((f32[2,1024,512]{1,2,0:T(8,128)}, f32[2,512,512]{1,2,0:T(8,128)}), (f32[2,1024,512]{1,2,0:T(8,128)}, f32[2,512,512]{1,2,0:T(8,128)})) %all-reduce.13.cloned.1.call-update) | async-done | bytes 6291472 | tf_op jit(solution)/shard_map/psum | solution.py:16
  620.2 3.3 broadcast_select_fusion.1
  624.3 14.4 %while.4 = (s32[]{:T(128)}, f32[2,512,512]{1,2,0:T(8,128)}, s32[4,2]{0,1:T(2,128)S(1)}, f32[4,2,128,128]{3,2,0,1:T(8,128)}, s32[]{:T(128)}) while((s32[]{:T(128)}, f32[2,512,512]{1,2,0:T(8,128)}, s32[4,2]{0,1:T(2,128)S(1)}, f32[4,2,128,128]{3,2,0,1:T(8,128)}, s32[]{:T(128)}) %tuple.74), condition=%wide.while_cond.2, body=%wide.while_body.2.sunk | while | flops 2 | bytes 787049 | solution.py:78
  624.9 2.3 constant_dynamic-slice_fusion.11
  628.5 2.3 constant_dynamic-slice_fusion.11
  632.2 2.3 constant_dynamic-slice_fusion.11
  635.8 2.2 constant_dynamic-slice_fusion.11
  638.8 80.4 %custom-call.45 = f32[2,4,128,128]{2,3,1,0:T(8,128)} custom-call(f32[2,4,128,128]{3,2,1,0:T(8,128)} %bitcast.113), custom_call_target="InvertDiagBlocksLowerTriangular" | custom-call | tf_op jit(solution)/shard_map/triangular_solve | solution.py:78
  719.2 3.3 fusion.41
  722.5 2.9 convolution_subtract_fusion
  727.5 3.4 fusion.19
  732.8 5.1 fusion.22
  743.8 3.3 fusion.7
  747.1 118.8 %all-reduce.15.cloned.1.call-done = (f32[2,512,512]{1,2,0:T(8,128)}, f32[512,2048]{1,0:T(8,128)}) async-done(((f32[2,512,512]{1,2,0:T(8,128)}, f32[512,2048]{1,0:T(8,128)}), (f32[2,512,512]{1,2,0:T(8,128)}, f32[512,2048]{1,0:T(8,128)})) %all-reduce.15.cloned.1.call-update) | async-done | bytes 6291472 | tf_op jit(solution)/shard_map/psum | solution.py:16
  865.9 18.0 %fusion.25 = f32[1024,2048]{1,0:T(8,128)} fusion(f32[512,2048]{1,0:T(8,128)} %get-tuple-element.73, f32[2,1024,512]{1,2,0:T(8,128)} %get-tuple-element.70), kind=kOutput, calls=%fused_computation.38 | convolution fusion | flops 12884901888 | bytes 14680064 | tf_op jit(solution)/shard_map/dot_general | solution.py:84
  883.9 8.8 convolution_subtract_fusion.1
  892.7 5.4 copy.82
  898.0 22.9 %subtract_select_fusion = f32[1024,2048]{1,0:T(8,128)} fusion(f32[1024,2048]{1,0:T(8,128)} %copy-done.2, f32[1024,2048]{1,0:T(8,128)} %fusion.25, f32[512,2048]{1,0:T(8,128)} %get-tuple-element.73, pred[1024]{0:T(1024)(128)(4,1)S(1)} %compare_and_fusion, pred[2048]{0:T(1024)(128)(4,1)S(1)} %eq.72, f32[2,1024,512]{1,2,0:T(8,128)} %get-tuple-element.70), kind=kOutput, calls=%fused_computation.7 | convolution fusion | flops 12891193344 | bytes 35654656 | tf_op jit(solution)/shard_map/dot_general | solution.py:85
  (144 shorter events, 46.2 us)
Async XLA Ops:
  8.0 2.3 copy-start
  8.0 38.7 %all-reduce.9.cloned.1.call-start = ((), (), s32[]{:S(2)}) async-start(), calls=%async_computation | async-start | bytes 524288 | tf_op jit(solution)/shard_map/psum | solution.py:16
  9.8 105.5 %all-reduce.11.cloned.1.call-start = ((), (), s32[]{:S(2)}) async-start(), calls=%async_computation.1 | async-start | bytes 4194304 | tf_op jit(solution)/shard_map/psum | solution.py:16
  10.3 38.5 %copy-start.9 = (pred[1024,512]{0,1:T(8,128)(4,1)}, pred[1024,512]{0,1:T(8,128)(4,1)S(1)}, u32[]{:S(2)}) copy-start(pred[1024,512]{0,1:T(8,128)(4,1)S(1)} %broadcast_compare_fusion) | copy-start | bytes 1572868
  48.8 2.0 copy-start.5
  52.5 360.2 %all-gather.2.cloned.1.call-start = ((), (), s32[]{:S(2)}) async-start(), calls=%async_computation.2 | async-start | bytes 1572864 | tf_op jit(solution)/shard_map/all_gather | solution.py:51
  53.1 567.1 %all-reduce.13.cloned.1.call-start = ((), (), s32[]{:S(2)}) async-start(), calls=%async_computation.3 | async-start | bytes 12582912 | tf_op jit(solution)/shard_map/psum | solution.py:16
  53.3 96.0 %copy-start.20 = (pred[128,128]{1,0:T(8,128)(4,1)}, pred[128,128]{1,0:T(8,128)(4,1)S(1)}, u32[]{:S(2)}) copy-start(pred[128,128]{1,0:T(8,128)(4,1)S(1)} %iota_compare_fusion.4) | copy-start | bytes 49156
  54.0 245.0 %copy-start.14 = (pred[512,512]{0,1:T(8,128)(4,1)}, pred[512,512]{0,1:T(8,128)(4,1)S(1)}, u32[]{:S(2)}) copy-start(pred[512,512]{0,1:T(8,128)(4,1)S(1)} %iota_compare_fusion.1) | copy-start | bytes 786436
  124.5 1.3 copy-start.8
  173.1 50.5 %copy-start.17 = (f32[2,384,128]{2,1,0:T(8,128)S(1)}, f32[2,384,128]{2,1,0:T(8,128)}, u32[]{:S(2)}) copy-start(f32[2,384,128]{2,1,0:T(8,128)} %convolution_subtract_fusion.3) | copy-start | bytes 1179652
  222.7 0.9 copy-start.19
  222.7 1.0 copy-start.22
  222.9 28.1 %copy-start.21 = (pred[128,128]{1,0:T(8,128)(4,1)S(1)}, pred[128,128]{1,0:T(8,128)(4,1)}, u32[]{:S(2)}) copy-start(pred[128,128]{1,0:T(8,128)(4,1)} %copy-done.20) | copy-start | bytes 49156
  223.6 74.3 %copy-start.23 = (pred[128,128]{1,0:T(8,128)(4,1)S(1)}, pred[128,128]{1,0:T(8,128)(4,1)}, u32[]{:S(2)}) copy-start(pred[128,128]{1,0:T(8,128)(4,1)} %iota_compare_fusion.5) | copy-start | bytes 49156
  224.1 1.3 copy-start.7
  397.5 3.6 copy-start.6
  411.8 0.7 copy-start.24
  411.9 1.1 copy-start.13
  411.9 454.0 %all-reduce.15.cloned.1.call-start = ((), (), s32[]{:S(2)}) async-start(), calls=%async_computation.4 | async-start | bytes 12582912 | tf_op jit(solution)/shard_map/psum | solution.py:16
  415.4 3.4 copy-start.2
  418.8 201.4 %copy-start.15 = (pred[512,512]{0,1:T(8,128)(4,1)S(1)}, pred[512,512]{0,1:T(8,128)(4,1)}, u32[]{:S(2)}) copy-start(pred[512,512]{0,1:T(8,128)(4,1)} %copy-done.14) | copy-start | bytes 786436
  719.2 3.3 copy-start.11
  722.5 3.0 copy-start.18
  725.5 2.0 copy-start.12
  739.9 2.2 copy-start.3
  865.9 18.0 %copy-start.4 = (f32[2,1024,512]{1,2,0:T(8,128)S(1)}, f32[2,1024,512]{1,2,0:T(8,128)}, u32[]{:S(2)}) copy-start(f32[2,1024,512]{1,2,0:T(8,128)} %get-tuple-element.70) | copy-start | bytes 12582916
  865.9 18.0 %copy-start.10 = (pred[1024,512]{0,1:T(8,128)(4,1)S(1)}, pred[1024,512]{0,1:T(8,128)(4,1)}, u32[]{:S(2)}) copy-start(pred[1024,512]{0,1:T(8,128)(4,1)} %copy-done.9) | copy-start | bytes 1572868
  865.9 18.0 %copy-start.16 = (f32[2,512,512]{1,2,0:T(8,128)S(1)}, f32[2,512,512]{1,2,0:T(8,128)}, u32[]{:S(2)}) copy-start(f32[2,512,512]{1,2,0:T(8,128)} %get-tuple-element.72) | copy-start | bytes 6291460
  898.0 22.9 %copy-start.1 = (f32[2,4]{1,0:T(2,128)S(1)}, f32[2,4]{1,0:T(2,128)}, u32[]{:S(2)}) copy-start(f32[2,4]{1,0:T(2,128)} %param.10) | copy-start | bytes 100
Sparse Core Ops, SparseCore 0:
  11.7 34.9 all-reduce.8
  52.6 62.5 all-reduce.10
  412.0 208.1 all-reduce.12
  747.2 118.6 all-reduce.14
Sparse Core Ops, SparseCore 1:
  54.5 24.2 all-gather.1
where the time goes:
time: 932 us; the launch traced here: 928 us
  waiting for transfers between devices  416 us (45%)
  other arithmetic  344 us (37%)
  matrix products  98.3 us (11%)
  local copies, waits for them, and re-layouts  53.7 us (6%)
  between operations  16.1 us (2%)
    psum x4, waiting for transfers between devices, spread(): return lax.psum(block, axis)  415 us
    another operation x16, other arithmetic, local(): factor = jnp.linalg.cholesky(diagonal)  158 us
    another operation x3, other arithmetic, local(): lax.linalg.triangular_solve(factor, block_sides, left_side=True, lower=True)  84.7 us
    another operation x3, other arithmetic, local(): lax.linalg.triangular_solve(factor, system_tiles, left_side=False, lower=...  78.9 us
    another operation x40, local copies, waits for them, and re-layouts  27.2 us
    dot_general x1, matrix products, local(): jnp.dot(panel[1], solved_sides, precision=lax.Precision.HIGHEST)  22.9 us
    another operation x7, matrix products, local(): lax.linalg.triangular_solve(factor, block_sides, left_side=True, lower=True)  20.6 us
  transfers between devices with their start and end apart: 5, of which 4 were waited for; matrix products, arithmetic and copies ran while one was open for 32% of the time, Pallas kernels for 0%

commit v1 on v0

v1 whole, which is shorter than its diff:
```python
import jax
import jax.numpy as jnp
from jax import lax
from jax.experimental import pallas as pl
from jax.experimental.pallas import tpu as pltpu
from jax.sharding import PartitionSpec as P

GROUP = 64
B = 128
F32 = jnp.float32
BF16 = jnp.bfloat16
HI = lax.Precision.HIGHEST
AXES = ("tm", "vox", "feat")
FIRST = (((0,), (0,)), ((), ()))


def lane_b(v, lane):
    return jnp.broadcast_to(v[:, lane : lane + 1], (8, B))


def sub_b(v, row):
    return jnp.broadcast_to(v[row : row + 1, :], (8, B))


def inverse_factors(tiles):
    n = B // 8
    lanes = lax.broadcasted_iota(jnp.int32, (8, B), 1)
    subs = lax.broadcasted_iota(jnp.int32, (8, B), 0)
    strips = [[t[8 * i : 8 * i + 8, :] for i in range(n)] for t in tiles]
    done = [[] for _ in tiles]
    for s in range(n):
        pivot_lanes = (lanes >= 8 * s) & (lanes < 8 * s + 8)
        for r in range(len(tiles)):
            st = strips[r]
            rows = [sub_b(st[s], k) for k in range(8)]
            e = [[lane_b(rows[k], 8 * s + j) if j >= k else None for j in range(8)] for k in range(8)]
            rows = [
                jnp.where(pivot_lanes, jnp.where(lanes == 8 * s + k, 1.0, 0.0), rows[k]) for k in range(8)
            ]
            m = {}
            recips = []
            for j in range(8):
                recip = 1.0 / e[j][j]
                recips.append(recip)
                for k in range(j + 1, 8):
                    m[k, j] = e[j][k] * recip
                    for l in range(k, 8):
                        e[k][l] = e[k][l] - m[k, j] * e[j][l]
                    rows[k] = rows[k] - m[k, j] * rows[j]
            out = jnp.zeros((8, B), F32)
            for k in range(8):
                out = jnp.where(subs == k, rows[k] * lax.rsqrt(e[k][k]), out)
            done[r].append(jnp.where(lanes < 8 * s + 8, out, 0.0))
            if s + 1 < n:
                v = [None] * 8
                for k in range(7, -1, -1):
                    acc = rows[k] * recips[k]
                    for l in range(k + 1, 8):
                        acc = acc - m[l, k] * v[l]
                    v[k] = acc
                for t in range(s + 1, n):
                    cols = [lane_b(st[t], 8 * s + j) for j in range(8)]
                    acc = jnp.where(pivot_lanes, 0.0, st[t])
                    for j in range(8):
                        acc = acc - cols[j] * v[j]
                    st[t] = acc
    return [jnp.concatenate(d, axis=0) for d in done]


def factor_kernel(weights_ref, x_ref, label_ref, w_ref, k_ref, m_ref):
    options, groups = weights_ref.shape
    time, width = x_ref.shape
    nk = width // B
    nm = (width + time) // B
    x = x_ref[...]
    row = lax.broadcasted_iota(jnp.int32, (B, B), 0)
    col = lax.broadcasted_iota(jnp.int32, (B, B), 1)
    eye = lax.broadcasted_iota(jnp.int32, (time, time), 0) == lax.broadcasted_iota(
        jnp.int32, (time, time), 1
    )
    eye = jnp.where(eye, 1.0, 0.0)
    gram = lax.dot_general(x, x, FIRST, preferred_element_type=F32) * (1.0 / time)
    xt = lax.dot_general(x, eye.astype(BF16), FIRST, preferred_element_type=F32) * time**-0.5
    for r in range(options):
        m_ref[r, :width, :width] = gram
        m_ref[r, :width, width:] = xt
        m_ref[r, width:, width:] = eye
        for k in range(nk):
            at = slice(k * B, (k + 1) * B)
            ridge = jnp.zeros((1, B), F32)
            for g in range(groups):
                ridge = jnp.where(label_ref[:, at] == g, weights_ref[r, g], ridge)
            m_ref[r, at, at] = gram[at, at] + jnp.where(row == col, ridge, 0.0)

    def step(k, _):
        at = pl.ds(pl.multiple_of(k * B, B), B)
        inverses = inverse_factors([m_ref[r, at, at] for r in range(options)])
        for r in range(options):
            m_ref[r, at, :] = jnp.dot(inverses[r], m_ref[r, at, :], precision=HI)

        def rest(j, _):
            to = pl.ds(pl.multiple_of(j * B, B), B)
            for r in range(options):
                m_ref[r, to, :] -= lax.dot_general(
                    m_ref[r, at, to], m_ref[r, at, :], FIRST, precision=HI, preferred_element_type=F32
                )
            return 0

        lax.fori_loop(k + 1, nm, rest, 0)
        return 0

    lax.fori_loop(0, nk, step, 0)
    for r in range(options):
        w_ref[r] = m_ref[r, :width, width:]
        k_ref[r] = m_ref[r, width:, width:]


def factor(weights, x, labels):
    time, width = x.shape
    options = weights.shape[0]
    n = time + width
    vmem = pl.BlockSpec(memory_space=pltpu.VMEM)
    return pl.pallas_call(
        factor_kernel,
        out_shape=(
            jax.ShapeDtypeStruct((options, width, time), F32),
            jax.ShapeDtypeStruct((options, time, time), F32),
        ),
        in_specs=[pl.BlockSpec(memory_space=pltpu.SMEM), vmem, vmem],
        out_specs=(vmem, vmem),
        scratch_shapes=[pltpu.VMEM((options, n, n), F32)],
        name="factor",
    )(weights, x, labels)


def split(v):
    high = v.astype(BF16)
    return high, (v - high.astype(F32)).astype(BF16)


def apply_kernel(
    place_ref, weights_ref, xt_ref, xc_ref, label_ref, choice_ref, w_ref, k_ref, *refs
):
    y_refs, (trail_ref, right_ref, khl_ref, y_ref) = refs[:-4], refs[-4:]
    options, groups = weights_ref.shape
    rows, time = xt_ref.shape
    width = xc_ref.shape[1]
    part = time // len(y_refs)
    step = pl.program_id(0)
    row_start, column_start, tm = place_ref[0], place_ref[1], place_ref[2]

    @pl.when(step == 0)
    def _():
        for r in range(options):
            khl_ref[r, 0], khl_ref[r, 1] = split(k_ref[r])

    def product(a_ref, b):
        return jnp.dot(a_ref[0], b, preferred_element_type=F32) + jnp.dot(
            a_ref[1], b, preferred_element_type=F32
        )

    def write(out_ref, z, scale):
        high, low = split(z * scale)
        xt = xt_ref[...]
        out_ref[...] = jnp.dot(xt, high, preferred_element_type=F32) + jnp.dot(
            xt, low, preferred_element_type=F32
        )

    @pl.when(step < options)
    def _():
        out_ref = trail_ref.at[0]

        @pl.when(column_start == 0)
        def _():
            out_ref[...] = jnp.zeros_like(out_ref)

        @pl.when(column_start > 0)
        def _():
            write(out_ref, product(khl_ref.at[step], xc_ref[...]), 1.0 / time)

            @pl.when((column_start >= row_start) & (column_start < row_start + rows))
            def _():
                at = pl.ds(pl.multiple_of(column_start - row_start, B), width)
                ridge = jnp.zeros((1, width), F32)
                for g in range(groups):
                    ridge = jnp.where(label_ref[...] == g, weights_ref[step, g], ridge)
                row = lax.broadcasted_iota(jnp.int32, (width, width), 0)
                col = lax.broadcasted_iota(jnp.int32, (width, width), 1)
                out_ref[at, :] += jnp.where(row == col, ridge, 0.0)

            @pl.when(row_start == 0)
            def _():
                out_ref[:width, :] = jnp.zeros((width, width), F32)

    @pl.when(step >= options)
    def _():
        n = len(y_refs)
        for s in range(n):
            at = pl.ds(pl.multiple_of(lax.rem(tm - s + n, n) * part, part), part)
            y_ref[at, :] = y_refs[s][...]
        y = y_ref[...]
        choice = choice_ref[...]
        z = product(khl_ref.at[0], y)
        for r in range(1, options):
            z = jnp.where(choice == r, product(khl_ref.at[r], y), z)
        write(right_ref, z, time**-0.5)

        @pl.when(row_start == 0)
        def _():
            for r in range(options):
                high, low = split(w_ref[r])
                v = jnp.dot(high, y, preferred_element_type=F32) + jnp.dot(
                    low, y, preferred_element_type=F32
                )
                solved = v if r == 0 else jnp.where(choice == r, v, solved)
            right_ref[:width, :] = solved


def apply(place, weights, xt, xc, labels, choice, w, k, ys):
    rows, time = xt.shape
    width = xc.shape[1]
    voxels = ys[0].shape[1]
    options = weights.shape[0]
    tile = min(512, voxels)
    smem = pl.BlockSpec(memory_space=pltpu.SMEM)
    vmem = pl.BlockSpec(memory_space=pltpu.VMEM)

    def along(s):
        return (0, jnp.maximum(s - options, 0))

    return pl.pallas_call(
        apply_kernel,
        grid=(options + voxels // tile,),
        out_shape=(
            jax.ShapeDtypeStruct((options, rows, width), F32),
            jax.ShapeDtypeStruct((rows, voxels), F32),
        ),
        in_specs=[smem, smem, vmem, vmem, vmem, pl.BlockSpec((1, tile), along), vmem, vmem]
        + [pl.BlockSpec((y.shape[0], tile), along) for y in ys],
        out_specs=(
            pl.BlockSpec((1, rows, width), lambda s: (jnp.minimum(s, options - 1), 0, 0)),
            pl.BlockSpec((rows, tile), along),
        ),
        scratch_shapes=[
            pltpu.VMEM((options, 2, time, time), BF16),
            pltpu.VMEM((time, tile), BF16),
        ],
        name="apply",
    )(place, weights, xt, xc, labels, choice, w, k, *ys)


def local(
    design_matrix, measured_signals, predictor_group_label, shrinkage_weights, target_shrink_choice
):
    nt, nv, nf = (lax.axis_size(a) for a in AXES)
    members = nt * nf
    tm, vox = lax.axis_index("tm"), lax.axis_index("vox")
    member = lax.axis_index(("tm", "feat"))
    rows = design_matrix.shape[1]
    width = predictor_group_label.shape[0]

    def device(g, v):
        return (g // nf * nv + v) * nf + g % nf

    def share(block, owner, mine):
        out = block
        for s in range(1, members):
            pairs = [(device(owner(v), v), device((owner(v) + s) % members, v)) for v in range(nv)]
            got = lax.ppermute(block, AXES, pairs)
            out = jnp.where((member - mine + members) % members == s, got, out)
        return out

    labels = predictor_group_label
    stride = nv
    while stride > 1:
        half = stride // 2
        got = lax.ppermute(labels, "vox", [(a, a + half) for a in range(0, nv, stride)])
        labels = jnp.where(vox % stride == half, got, labels)
        stride = half

    first = share(design_matrix[:, :width], lambda v: 0, 0)
    source = vox * width // rows
    own = lax.dynamic_slice_in_dim(design_matrix, vox * width - source * rows, width, 1)
    columns = share(own, lambda v: v * width // rows, source)
    ys = [measured_signals]
    for s in range(1, nt):
        ys.append(lax.ppermute(measured_signals, "tm", [(a, (a + s) % nt) for a in range(nt)]))

    w, k = factor(shrinkage_weights, first, labels[None, :])
    place = jnp.stack([member * rows, vox * width, tm]).astype(jnp.int32)
    choice = jnp.repeat(target_shrink_choice, GROUP)[None, :]
    return apply(
        place,
        shrinkage_weights,
        design_matrix.T,
        columns,
        predictor_group_label[None, :],
        choice,
        w,
        k,
        ys,
    )


def solution(mesh):
    return jax.shard_map(
        local,
        mesh=mesh,
        in_specs=(P(None, ("tm", "feat")), P("tm", "vox"), P("vox"), P(), P("vox")),
        out_specs=(P(None, ("tm", "feat"), "vox"), P(("tm", "feat"), "vox")),
        check_vma=False,
    )
```

time: 932 us -> 98.2 us (0.11)
  waiting for transfers between devices: 416 us -> 2.65 us
  other arithmetic: 344 us -> 4.64 us
  matrix products: 98.3 us -> 0 us
  Pallas kernels: 0 us -> 65.4 us
  local copies, waits for them, and re-layouts: 53.7 us -> 5.24 us
  starting transfers between devices: 0.21 us -> 18.5 us
  between operations: 16.1 us -> 0.84 us
    psum x4 -> x0, waiting for transfers between devices: 415 us -> none  [spread(): return lax.psum(block, axis)]
    another operation x22 -> x1, other arithmetic: 321 us -> 0.67 us  [local(): place = jnp.stack([member * rows, vox * width, tm]).astype(jnp.int32)]
    pallas_call x0 -> x2, Pallas kernels: none -> 65.4 us  [the longest x1 52.2 us: factor(): pl.pallas_call(factor_kernel, out_shape=(jax.ShapeDtypeStruct((options, w...]
    dot_general x6 -> x0, matrix products: 54.8 us -> none  [the longest x1 22.9 us: local(): jnp.dot(panel[1], solved_sides, precision=lax.Precision.HIGHEST)]
    another operation x20 -> x0, matrix products: 43.4 us -> none  [the longest x7 20.6 us: local(): lax.linalg.triangular_solve(factor, block_sides, left_side=True, lower=True)]
    another operation x55 -> x1, local copies, waits for them, and re-layouts: 33.5 us -> 0.67 us  [local(): choice = jnp.repeat(target_shrink_choice, GROUP)[None, :]]
    ppermute x0 -> x10, starting transfers between devices: none -> 18.5 us  [the longest x6 11.4 us: share(): got = lax.ppermute(block, AXES, pairs)]
    select_n x7 -> x5, other arithmetic: 18.9 us -> 3.98 us  [the longest x2 2.71 us: share(): out = jnp.where((member - mine + members) % members == s, got, out)]
  transfers between devices with their start and end apart: 5 -> 10, of which waited for: 4 -> 2; matrix products, arithmetic and copies ran while one was open for 32% -> 8% of each run, Pallas kernels for 0% -> 54%
where the time goes in v1:
time: 98.2 us; the launch traced here: 97.3 us
  Pallas kernels  65.4 us (67%)
  starting transfers between devices  18.5 us (19%)
  local copies, waits for them, and re-layouts  5.24 us (5%)
  other arithmetic  4.64 us (5%)
  waiting for transfers between devices  2.65 us (3%)
    pallas_call x1, Pallas kernels, factor(): pl.pallas_call(factor_kernel, out_shape=(jax.ShapeDtypeStruct((options, w...  52.2 us
    pallas_call x1, Pallas kernels, apply(): pl.pallas_call(apply_kernel, grid=(options + voxels // tile,), out_shape=...  13.2 us
    ppermute x6, starting transfers between devices, share(): got = lax.ppermute(block, AXES, pairs)  11.4 us
    ppermute x3, starting transfers between devices, local(): lax.ppermute(labels, 'vox', [(a, a + half) for a in range(0, nv, stride)])  7.05 us
    unnamed x3, local copies, waits for them, and re-layouts  2.87 us
    select_n x2, other arithmetic, share(): out = jnp.where((member - mine + members) % members == s, got, out)  2.71 us
    ppermute x3, waiting for transfers between devices, local(): lax.ppermute(labels, 'vox', [(a, a + half) for a in range(0, nv, stride)])  2.63 us
  transfers between devices with their start and end apart: 10, of which 2 were waited for; matrix products, arithmetic and copies ran while one was open for 8% of the time, Pallas kernels for 54%

profile of v1, /device:TPU:0, one launch (start us, length us, event | category | flops | bytes accessed | tf_op | source)
XLA Modules:
  0.0 97.3 jit_solution(7390167422913203052)
XLA Ops:
  0.6 1.0 slice.3
  1.6 2.4 %collective-permute-start.5 = (bf16[256,512]{1,0:T(8,128)(2,1)S(1)}, bf16[256,512]{1,0:T(8,128)(2,1)S(1)}, u32[]{:S(2)}, u32[]{:S(2)}) collective-permute-start(bf16[256,512]{1,0:T(8,128)(2,1)S(1)} %slice.3), channel_id=1, source_target_pairs={{0,1},{2,3},{4,5},{6,7},{8,9},{10,11},{12,13},{14,15}} | collective-permute-start | bytes 786440 | tf_op jit(solution)/shard_map/ppermute | solution.py:269
  4.0 3.2 %collective-permute-start.4 = (bf16[256,512]{1,0:T(8,128)(2,1)S(1)}, bf16[256,512]{1,0:T(8,128)(2,1)S(1)}, u32[]{:S(2)}, u32[]{:S(2)}) collective-permute-start(bf16[256,512]{1,0:T(8,128)(2,1)S(1)} %slice.3), channel_id=1, source_target_pairs={{0,16},{2,18},{4,20},{6,22},{8,24},{10,26},{12,28},{14,30}} | collective-permute-start | bytes 786440 | tf_op jit(solution)/shard_map/ppermute | solution.py:269
  7.2 1.3 %collective-permute-start.3 = (bf16[256,512]{1,0:T(8,128)(2,1)S(1)}, bf16[256,512]{1,0:T(8,128)(2,1)S(1)}, u32[]{:S(2)}, u32[]{:S(2)}) collective-permute-start(bf16[256,512]{1,0:T(8,128)(2,1)S(1)} %slice.3), channel_id=1, source_target_pairs={{0,17},{2,19},{4,21},{6,23},{8,25},{10,27},{12,29},{14,31}} | collective-permute-start | bytes 786440 | tf_op jit(solution)/shard_map/ppermute | solution.py:269
  8.5 4.5 %collective-permute-start.6 = (s32[512]{0:T(512)}, s32[512]{0:T(512)S(1)}, u32[]{:S(2)}, u32[]{:S(2)}) collective-permute-start(s32[512]{0:T(512)} %param.7), channel_id=1, source_target_pairs={{0,8},{1,9},{16,24},{17,25}} | collective-permute-start | bytes 6152 | tf_op jit(solution)/shard_map/ppermute | solution.py:277
  13.0 0.1 collective-permute-start.9
  13.1 1.4 %collective-permute-done.6 = s32[512]{0:T(512)S(1)} collective-permute-done((s32[512]{0:T(512)}, s32[512]{0:T(512)S(1)}, u32[]{:S(2)}, u32[]{:S(2)}) %collective-permute-start.6) | collective-permute-done | bytes 2080 | tf_op jit(solution)/shard_map/ppermute | solution.py:277
  14.5 0.7 broadcast_select_fusion
  15.2 1.3 %collective-permute-start.7 = (s32[512]{0:T(512)S(1)}, s32[512]{0:T(512)S(1)}, u32[]{:S(2)}, u32[]{:S(2)}) collective-permute-start(s32[512]{0:T(512)S(1)} %broadcast_select_fusion), channel_id=1, source_target_pairs={{0,4},{8,12},{1,5},{9,13},{16,20},{24,28},{17,21},{25,29}} | collective-permute-start | bytes 6152 | tf_op jit(solution)/shard_map/ppermute | solution.py:277
  16.5 1.2 %collective-permute-done.7 = s32[512]{0:T(512)S(1)} collective-permute-done((s32[512]{0:T(512)S(1)}, s32[512]{0:T(512)S(1)}, u32[]{:S(2)}, u32[]{:S(2)}) %collective-permute-start.7) | collective-permute-done | bytes 2080 | tf_op jit(solution)/shard_map/ppermute | solution.py:277
  17.8 1.3 %collective-permute-start.8 = (s32[512]{0:T(512)S(1)}, s32[512]{0:T(512)S(1)}, u32[]{:S(2)}, u32[]{:S(2)}) collective-permute-start(s32[512]{0:T(512)S(1)} %broadcast_select_fusion.1), channel_id=1, source_target_pairs={{0,2},{4,6},{8,10},{12,14},{1,3},{5,7},{9,11},{13,15},{16,18},{20,... | collective-permute-start | bytes 6152 | tf_op jit(solution)/shard_map/ppermute | solution.py:277
  19.1 0.0 collective-permute-done.5
  19.1 0.0 collective-permute-done.4
  19.1 0.0 collective-permute-done.3
  19.1 1.9 %select_select_fusion = (bf16[256,512]{1,0:T(8,128)(2,1)}, bf16[256,512]{1,0:T(8,128)(2,1)S(1)}) fusion(bf16[256,512]{1,0:T(8,128)(2,1)S(1)} %collective-permute-done.3, bf16[256,512]{1,0:T(8,128)(2,1)S(1)} %collective-permute-done.4, bf16[256,512]{1,0:T(8,128)(2,1)S(1)} %collective-permute-done.5, pred[]{:T(512)S(6)} %eq.42, pred[]{:T(512)S(6)} %eq.41, ...), kind=kLoop, calls=%fused_computation | loop fusion | flops 393216 | bytes 1835015 | tf_op jit(solution)/shard_map/jit(_where)/select_n | solution.py:270
  21.0 1.3 %collective-permute-start.2 = (bf16[256,512]{1,0:T(8,128)(2,1)S(1)}, bf16[256,512]{1,0:T(8,128)(2,1)S(1)}, u32[]{:S(2)}, u32[]{:S(2)}) collective-permute-start(bf16[256,512]{1,0:T(8,128)(2,1)S(1)} %get-tuple-element.7), channel_id=1, source_target_pairs={{0,1},{2,3},{5,20},{7,22},{24,25},{26,27},{29,12},{31,14}} | collective-permute-start | bytes 786440 | tf_op jit(solution)/shard_map/ppermute | solution.py:269
  22.3 1.9 %collective-permute-start.1 = (bf16[256,512]{1,0:T(8,128)(2,1)S(1)}, bf16[256,512]{1,0:T(8,128)(2,1)S(1)}, u32[]{:S(2)}, u32[]{:S(2)}) collective-permute-start(bf16[256,512]{1,0:T(8,128)(2,1)S(1)} %get-tuple-element.7), channel_id=1, source_target_pairs={{0,16},{2,18},{5,21},{7,23},{24,8},{26,10},{29,13},{31,15}} | collective-permute-start | bytes 786440 | tf_op jit(solution)/shard_map/ppermute | solution.py:269
  24.2 1.3 %collective-permute-start = (bf16[256,512]{1,0:T(8,128)(2,1)S(1)}, bf16[256,512]{1,0:T(8,128)(2,1)S(1)}, u32[]{:S(2)}, u32[]{:S(2)}) collective-permute-start(bf16[256,512]{1,0:T(8,128)(2,1)S(1)} %get-tuple-element.7), channel_id=1, source_target_pairs={{0,17},{2,19},{5,4},{7,6},{24,9},{26,11},{29,28},{31,30}} | collective-permute-start | bytes 786440 | tf_op jit(solution)/shard_map/ppermute | solution.py:269
  25.5 0.7 pad_add_fusion.place_ref
  26.2 2.1 %copy.7 = bf16[256,1024]{0,1:T(8,128)(2,1)} copy(bf16[256,1024]{1,0:T(8,128)(2,1)} %param.5) | data formatting | bytes 1048576 | tf_op args[0]
  28.3 0.7 broadcast_in_dim.10
  29.0 0.7 broadcast_in_dim_reshape.3.choice_ref
  29.7 0.0 collective-permute-done.8
  29.7 0.6 broadcast_select_fusion.2
  30.3 52.2 %factor.1 = (f32[2,512,256]{2,1,0:T(8,128)}, f32[2,256,256]{2,1,0:T(8,128)}) custom-call(f32[2,4]{1,0:T(2,128)} %weights_ref.3, bf16[256,512]{1,0:T(8,128)(2,1)} %get-tuple-element.6.x_ref, s32[1,512]{1,0:T(1,128)} %bitcast.8), custom_call_target="tpu_custom_call" | custom-call | tf_op jit(solution)/shard_map/factor/pallas_call | solution.py:123
  82.5 0.0 collective-permute-done.2
  82.5 0.0 collective-permute-done.1
  82.5 0.0 collective-permute-done
  82.5 0.8 select_select_fusion.1.xc_ref
  83.3 0.0 collective-permute-done.9.refs_1_
  83.3 0.0 copy-start
  83.3 0.8 copy-done
  84.1 13.2 %apply.1 = (f32[2,1024,512]{2,1,0:T(8,128)}, f32[1024,2048]{1,0:T(8,128)}) custom-call(s32[3]{0:T(128)} %pad_add_fusion.place_ref, f32[2,4]{1,0:T(2,128)} %weights_ref.3, bf16[1024,256]{1,0:T(8,128)(2,1)} %bitcast.6, bf16[256,512]{1,0:T(8,128)(2,1)} %select_select_fusion.1.xc_ref, s32[1,512]{1,0:T(1,128)} %bitcast.7, ...), custom_call_target="tpu_custom_call" | custom-call | tf_op jit(solution)/shard_map/apply/pallas_call | solution.py:231
  (1 shorter events, 0.0 us)
Async XLA Ops:
  1.6 17.5 %collective-permute-start.5 = (bf16[256,512]{1,0:T(8,128)(2,1)S(1)}, bf16[256,512]{1,0:T(8,128)(2,1)S(1)}, u32[]{:S(2)}, u32[]{:S(2)}) collective-permute-start(bf16[256,512]{1,0:T(8,128)(2,1)S(1)} %slice.3), channel_id=1, source_target_pairs={{0,1},{2,3},{4,5},{6,7},{8,9},{10,11},{12,13},{14,15}} | collective-permute-start | bytes 786440 | tf_op jit(solution)/shard_map/ppermute | solution.py:269
  4.0 15.0 %collective-permute-start.4 = (bf16[256,512]{1,0:T(8,128)(2,1)S(1)}, bf16[256,512]{1,0:T(8,128)(2,1)S(1)}, u32[]{:S(2)}, u32[]{:S(2)}) collective-permute-start(bf16[256,512]{1,0:T(8,128)(2,1)S(1)} %slice.3), channel_id=1, source_target_pairs={{0,16},{2,18},{4,20},{6,22},{8,24},{10,26},{12,28},{14,30}} | collective-permute-start | bytes 786440 | tf_op jit(solution)/shard_map/ppermute | solution.py:269
  7.2 11.9 %collective-permute-start.3 = (bf16[256,512]{1,0:T(8,128)(2,1)S(1)}, bf16[256,512]{1,0:T(8,128)(2,1)S(1)}, u32[]{:S(2)}, u32[]{:S(2)}) collective-permute-start(bf16[256,512]{1,0:T(8,128)(2,1)S(1)} %slice.3), channel_id=1, source_target_pairs={{0,17},{2,19},{4,21},{6,23},{8,25},{10,27},{12,29},{14,31}} | collective-permute-start | bytes 786440 | tf_op jit(solution)/shard_map/ppermute | solution.py:269
  8.5 6.0 %collective-permute-start.6 = (s32[512]{0:T(512)}, s32[512]{0:T(512)S(1)}, u32[]{:S(2)}, u32[]{:S(2)}) collective-permute-start(s32[512]{0:T(512)} %param.7), channel_id=1, source_target_pairs={{0,8},{1,9},{16,24},{17,25}} | collective-permute-start | bytes 6152 | tf_op jit(solution)/shard_map/ppermute | solution.py:277
  13.0 70.3 %collective-permute-start.9 = (bf16[128,2048]{1,0:T(8,128)(2,1)}, bf16[128,2048]{1,0:T(8,128)(2,1)S(1)}, u32[]{:S(2)}, u32[]{:S(2)}) collective-permute-start(bf16[128,2048]{1,0:T(8,128)(2,1)} %refs_0_.1), channel_id=1, source_target_pairs={{0,16},{16,0},{1,17},{17,1},{2,18},{18,2},{3,19},{19,3},{4,20},{20... | collective-permute-start | bytes 1572872 | tf_op jit(solution)/shard_map/ppermute | solution.py:287
  15.2 2.6 %collective-permute-start.7 = (s32[512]{0:T(512)S(1)}, s32[512]{0:T(512)S(1)}, u32[]{:S(2)}, u32[]{:S(2)}) collective-permute-start(s32[512]{0:T(512)S(1)} %broadcast_select_fusion), channel_id=1, source_target_pairs={{0,4},{8,12},{1,5},{9,13},{16,20},{24,28},{17,21},{25,29}} | collective-permute-start | bytes 6152 | tf_op jit(solution)/shard_map/ppermute | solution.py:277
  17.8 11.9 %collective-permute-start.8 = (s32[512]{0:T(512)S(1)}, s32[512]{0:T(512)S(1)}, u32[]{:S(2)}, u32[]{:S(2)}) collective-permute-start(s32[512]{0:T(512)S(1)} %broadcast_select_fusion.1), channel_id=1, source_target_pairs={{0,2},{4,6},{8,10},{12,14},{1,3},{5,7},{9,11},{13,15},{16,18},{20,... | collective-permute-start | bytes 6152 | tf_op jit(solution)/shard_map/ppermute | solution.py:277
  21.0 61.4 %collective-permute-start.2 = (bf16[256,512]{1,0:T(8,128)(2,1)S(1)}, bf16[256,512]{1,0:T(8,128)(2,1)S(1)}, u32[]{:S(2)}, u32[]{:S(2)}) collective-permute-start(bf16[256,512]{1,0:T(8,128)(2,1)S(1)} %get-tuple-element.7), channel_id=1, source_target_pairs={{0,1},{2,3},{5,20},{7,22},{24,25},{26,27},{29,12},{31,14}} | collective-permute-start | bytes 786440 | tf_op jit(solution)/shard_map/ppermute | solution.py:269
  22.3 60.1 %collective-permute-start.1 = (bf16[256,512]{1,0:T(8,128)(2,1)S(1)}, bf16[256,512]{1,0:T(8,128)(2,1)S(1)}, u32[]{:S(2)}, u32[]{:S(2)}) collective-permute-start(bf16[256,512]{1,0:T(8,128)(2,1)S(1)} %get-tuple-element.7), channel_id=1, source_target_pairs={{0,16},{2,18},{5,21},{7,23},{24,8},{26,10},{29,13},{31,15}} | collective-permute-start | bytes 786440 | tf_op jit(solution)/shard_map/ppermute | solution.py:269
  24.2 58.3 %collective-permute-start = (bf16[256,512]{1,0:T(8,128)(2,1)S(1)}, bf16[256,512]{1,0:T(8,128)(2,1)S(1)}, u32[]{:S(2)}, u32[]{:S(2)}) collective-permute-start(bf16[256,512]{1,0:T(8,128)(2,1)S(1)} %get-tuple-element.7), channel_id=1, source_target_pairs={{0,17},{2,19},{5,4},{7,6},{24,9},{26,11},{29,28},{31,30}} | collective-permute-start | bytes 786440 | tf_op jit(solution)/shard_map/ppermute | solution.py:269
  83.3 0.8 copy-start
